TPU v7x, 256 devices: a whole 4x4x8 slice. The times are simulated.
256 devices in a mesh: seq: 32 (over y, z), head: 8 (over x, core).
Axes of the slice: x: 4, y: 4, z: 8, core: 2. Of those that a mesh axis runs over, the one named last changes fastest.
Arguments:
- queries: bfloat16 [8192, 32, 128], P('seq', 'head'), may hold values from -42 to 42, as said below
- keys: bfloat16 [8192, 8, 128], P('seq', 'head'), may hold values from -6 to 6
- values: bfloat16 [8192, 8, 128], P('seq', 'head'), may hold values from -6 to 6
- feat_q: bfloat16 [32, 128, 128], P('head'), may hold values from -0.5 to 0.5
- feat_k: bfloat16 [32, 128, 128], P('head'), may hold values from -0.5 to 0.5
- samples: int32 [32], replicated, may hold values from 0 to 1
Outputs:
- student: bfloat16 [8192, 32, 128], P('seq', 'head')
- teacher: float32 [32, 128, 32, 128], P('seq', None, 'head')
- loss: float32 [], replicated
Inputs may be any that keep to these rules, and one draw needn't show every extreme that they name: `queries`: query vectors; some may be large multiples of earlier key vectors.
All inputs are finite; a program needn't handle non-finite values.
Results may differ from a plain program's by a relative error of at most 0.009.
Values may be sent and summed in bfloat16 or wider, within the bound.
No kernel may reach another device: no remote copies, remote signals or barrier semaphores. Data moves between devices by JAX's collectives and lax.ppermute only.
A program may use at most 64 MiB of HBM per device.

v0:
```python
import jax
import jax.numpy as jnp
from jax import lax
from jax.sharding import PartitionSpec as P

HD = 128
FEAT = 128
QH_DEV = 4
BLOCK = 128
PRECISE = lax.Precision.HIGHEST
MASKED = -1e30


def prefix(x, axis, combine, identity):
    count, mine = (lax.axis_size(axis), lax.axis_index(axis))
    everything = jax.tree.map(
        lambda part, kind: lax.all_gather(part.astype(kind), axis), x, (jnp.bfloat16, jnp.bfloat16)
    )
    start = jax.tree.map(
        lambda part, zero: jnp.broadcast_to(jnp.asarray(zero, part.dtype), part.shape), x, identity
    )

    def lap(k, before):
        reached = k < mine
        new = combine(
            before, jax.tree.map(lambda part, own: part[k].astype(own.dtype), everything, x)
        )
        return jax.tree.map(lambda a, b: jnp.where(reached, a, b), new, before)

    return lax.fori_loop(0, count, lap, start)


def features(logits):
    return jnp.concatenate(
        [jax.nn.softmax(logits, axis=-1), jax.nn.softmax(-logits, axis=-1)], axis=-1
    ).astype(jnp.bfloat16)


def add_pair(earlier, later):
    return (earlier[0] + later[0], earlier[1] + later[1])


def absorb(running, query_rows, row_places, key_part, value_part, inv_root):
    best, totals, accum = running
    scores = (
        jnp.einsum("bhd,kd->hbk", query_rows, key_part, preferred_element_type=jnp.float32)
        * inv_root
    )
    key_places = jnp.arange(key_part.shape[0])
    live = (key_places[None, :] <= row_places[:, None])[None]
    peak = jnp.max(jnp.where(live, scores, MASKED), axis=-1)
    newtop = jnp.maximum(best, peak)
    weights = jnp.where(live, jnp.exp(scores - newtop[..., None]), 0.0)
    totals = jnp.sum(weights, axis=-1)
    accum = jnp.einsum(
        "hbk,kd->hbd", weights.astype(jnp.bfloat16), value_part, preferred_element_type=jnp.float32
    )
    return (newtop, totals, accum)


def on_device(queries, keys, values, feat_q, feat_k, samples):
    tok_rows, head_count, head_width = queries.shape
    stretch_count = lax.axis_size("seq")
    inv_root = 1.0 / head_width**0.5
    key_rows = keys[:, 0]
    value_rows = values[:, 0]
    phi_q = features(
        jnp.einsum("lhd,hdf->lhf", queries, feat_q, preferred_element_type=jnp.float32)
    )
    phi_k = features(
        jnp.einsum("ld,hdf->lhf", key_rows, feat_k, preferred_element_type=jnp.float32)
    )
    span_rows = min(tok_rows, 512)
    block_count = tok_rows // span_rows
    fq_blocks = phi_q.reshape(block_count, span_rows, head_count, 2 * FEAT)
    fk_blocks = phi_k.reshape(block_count, span_rows, head_count, 2 * FEAT)
    value_blocks = value_rows.reshape(block_count, span_rows, head_width)
    block_states = jnp.einsum(
        "nlhf,nld->nhfd", fk_blocks, value_blocks, preferred_element_type=jnp.float32
    )
    block_totals = jnp.sum(fk_blocks, axis=1, dtype=jnp.float32)
    local_state = jnp.sum(block_states, axis=0)
    local_total = jnp.sum(block_totals, axis=0)
    empty_state = jnp.zeros_like(local_state)
    empty_total = jnp.zeros_like(local_total)
    enter_state, enter_total = prefix(
        (local_state, local_total), "seq", add_pair, (empty_state, empty_total)
    )
    before_states = jnp.cumsum(block_states, axis=0) - block_states
    before_totals = jnp.cumsum(block_totals, axis=0) - block_totals
    states_in = enter_state[None] + before_states
    totals_in = enter_total[None] + before_totals
    causal = jnp.arange(span_rows)[:, None] >= jnp.arange(span_rows)[None, :]
    kernel = jnp.einsum("nihf,njhf->nhij", fq_blocks, fk_blocks, preferred_element_type=jnp.float32)
    kernel = jnp.where(causal[None, None], kernel, 0.0)
    kernel_low = kernel.astype(jnp.bfloat16)
    numer = jnp.einsum(
        "nhij,njd->nihd", kernel_low, value_blocks, preferred_element_type=jnp.float32
    )
    numer = numer + jnp.einsum(
        "nihf,nhfd->nihd",
        fq_blocks,
        states_in,
        precision=PRECISE,
        preferred_element_type=jnp.float32,
    )
    denom = jnp.transpose(jnp.sum(kernel, axis=3), (0, 2, 1)) + jnp.einsum(
        "nihf,nhf->nih", fq_blocks, totals_in, precision=PRECISE, preferred_element_type=jnp.float32
    )
    student = (
        (numer / denom[..., None]).astype(jnp.bfloat16).reshape(tok_rows, head_count, head_width)
    )
    device_index = lax.axis_index("seq")
    picked = samples[device_index]
    row_first = device_index * tok_rows + picked * BLOCK
    query_rows = lax.dynamic_slice_in_dim(queries, picked * BLOCK, BLOCK, 0)
    row_places = row_first + jnp.arange(BLOCK)
    fresh = (
        jnp.full((head_count, BLOCK), MASKED, jnp.float32),
        jnp.zeros((head_count, BLOCK), jnp.float32),
        jnp.zeros((head_count, BLOCK, head_width), jnp.float32),
    )
    key_part = lax.all_gather(keys, "seq", axis=0, tiled=True)
    value_part = lax.all_gather(values, "seq", axis=0, tiled=True)
    best, totals, accum = lax.cond(
        jnp.int32(0) <= row_first + BLOCK - 1,
        lambda kept: absorb(
            kept, query_rows, row_places, key_part[:, 0], value_part[:, 0], inv_root
        ),
        lambda kept: kept,
        fresh,
    )
    mixed = accum / totals[..., None]
    teacher = jnp.transpose(mixed, (1, 0, 2))[None]
    student_rows = lax.dynamic_slice_in_dim(student, picked * BLOCK, BLOCK, 0).astype(jnp.float32)
    gap = student_rows - teacher[0]
    entry_count = stretch_count * lax.axis_size("head") * BLOCK * QH_DEV * HD
    loss = lax.psum(jnp.sum(gap * gap), ("seq", "head")) / entry_count
    return (student, teacher, loss)


def solution(mesh):
    in_specs = (
        P("seq", "head", None),
        P("seq", "head", None),
        P("seq", "head", None),
        P("head", None, None),
        P("head", None, None),
        P(),
    )
    out_specs = (P("seq", "head", None), P("seq", None, "head", None), P())
    return jax.shard_map(
        on_device, mesh=mesh, in_specs=in_specs, out_specs=out_specs, check_vma=False
    )
```

profile of v0, /device:TPU:1, one launch (start us, length us, event | category | flops | bytes accessed | tf_op | source)
XLA Modules:
  0.0 396.0 jit_solution(10727178128986259759)
XLA Ops:
  12.6 1.8 fusion.65
  14.5 1.3 dynamic_slice.26
  16.7 42.3 %all-gather.2 = bf16[32,4,256]{2,1,0:T(4,128)(2,1)S(1)} all-gather(bf16[1,4,256]{2,1,0:T(4,128)(2,1)S(1)} %convert_bitcast_fusion), channel_id=3, replica_groups=mesh['seq'=32,'head'=8] {'seq'}, dimensions={0}, use_global_device_ids=true | all-gather | bytes 67584 | tf_op jit(solution)/shard_map/all_gather | solution.py:17
  59.1 1.3 fusion.66
  60.4 1.3 fusion.69
  62.2 25.6 %all-gather.7.cloned.1.call-done = bf16[8192,1,128]{2,0,1:T(8,128)(2,1)} async-done(((bf16[256,1,128]{2,0,1:T(8,128)(2,1)}), bf16[8192,1,128]{2,0,1:T(8,128)(2,1)}) %all-gather.7.cloned.1.call-update) | async-done | bytes 2097168 | tf_op jit(solution)/shard_map/all_gather | solution.py:123
  87.8 77.7 %all-gather.9.cloned.1.call-done = bf16[8192,1,128]{2,0,1:T(8,128)(2,1)} async-done(((bf16[256,1,128]{2,0,1:T(8,128)(2,1)}), bf16[8192,1,128]{2,0,1:T(8,128)(2,1)}) %all-gather.9.cloned.1.call-update) | async-done | bytes 2097168 | tf_op jit(solution)/shard_map/all_gather | solution.py:124
  165.5 16.0 %conditional.1 = (f32[4,128]{1,0:T(4,128)S(1)}, f32[4,128,128]{2,1,0:T(8,128)S(1)}) conditional(s32[]{:T(128)} %convert_element_type.94, () %tuple.33, (s32[]{:T(128)}, s32[128]{0:T(128)S(1)}, bf16[256,4,128]{2,1,0:T(4,128)(2,1)}, s32[]{:T(128)}, bf16[8192,1,128]{2,0,1:T(8,128)(2,1)}, /*index=5*/bf16[8192,1,128]{2,0,1:T(8,128)(2,1)}) %tuple.34), branch_computations={%region_12.13_spmd, %region_13.0_spmd} | conditional | flops 2194669056 | bytes 59651608 | solution.py:125
  167.2 4.8 %fusion = (f32[4,128]{1,0:T(4,128)S(1)}, f32[128,4,8192]{2,0,1:T(8,128)S(1)}) fusion(pred[128,8192]{1,0:T(8,128)(4,1)S(1)} %iota_compare_fusion, bf16[8192,1,128]{2,0,1:T(8,128)(2,1)} %get-tuple-element.140, bf16[256,4,128]{2,0,1:T(8,128)(2,1)S(1)} %copy.30, s32[]{:T(128)} %get-tuple-element.139), kind=kOutput, calls=%fused_computation.2 | convolution fusion | flops 1086324224 | bytes 20056068 | tf_op jit(solution)/shard_map/cond/branch_1_fun/bhd,kd->hbk/dot_general | solution.py:46
  172.0 4.8 %fusion.5 = f32[4,128,128]{2,1,0:T(8,128)S(1)} fusion(f32[128,4,8192]{2,0,1:T(8,128)S(1)} %get-tuple-element.205, f32[4,128]{1,0:T(4,128)S(1)} %broadcast_maximum_fusion, pred[128,8192]{1,0:T(8,128)(4,1)S(1)} %iota_compare_fusion, bf16[8192,1,128]{2,0,1:T(8,128)(2,1)} %get-tuple-element.141), kind=kOutput, calls=%fused_computation.7 | convolution fusion | flops 1090519040 | bytes 20187136 | tf_op jit(solution)/shard_map/cond/branch_1_fun/hbk,kd->hbd/dot_general | solution.py:55
  176.8 4.6 %fusion.4 = f32[4,128]{1,0:T(4,128)S(1)} fusion(f32[128,4,8192]{2,0,1:T(8,128)S(1)} %get-tuple-element.205, f32[4,128]{1,0:T(4,128)S(1)} %broadcast_maximum_fusion, pred[128,8192]{1,0:T(8,128)(4,1)S(1)} %iota_compare_fusion), kind=kLoop, calls=%fused_computation.6 | loop fusion | flops 16776704 | bytes 17829888 | tf_op jit(solution)/shard_map/cond/branch_1_fun/reduce_sum | solution.py:54
  181.6 86.1 %all-gather.11.cloned.1.call-done = bf16[128,256,128]{2,1,0:T(8,128)(2,1)} async-done(((bf16[4,256,128]{2,1,0:T(8,128)(2,1)}), bf16[128,256,128]{2,1,0:T(8,128)(2,1)}) %all-gather.11.cloned.1.call-update) | async-done | bytes 8388624 | tf_op jit(solution)/shard_map/all_gather | solution.py:17
  267.6 40.8 %while.16 = (s32[]{:T(128)}, f32[4,256,128]{2,1,0:T(8,128)S(1)}, f32[4,256]{1,0:T(4,128)S(1)}, s32[]{:T(128)}, bf16[32,4,256,128]{3,2,1,0:T(8,128)(2,1)}, /*inde...) while((s32[]{:T(128)}, f32[4,256,128]{2,1,0:T(8,128)S(1)}, f32[4,256]{1,0:T(4,128)S(1)}, ...), condition=%wide.region_10.0_spmd.clone, body=%wide.region_9.0_spmd.clone.sunk | while | flops 528388 | bytes 1321083 | solution.py:30
  268.9 1.2 add_select_fusion.4
  270.2 1.2 add_select_fusion.4
  271.5 1.2 add_select_fusion.4
  272.7 1.2 add_select_fusion.4
  279.1 1.2 add_select_fusion.4
  281.7 1.2 add_select_fusion.4
  284.2 1.2 add_select_fusion.4
  286.8 1.2 add_select_fusion.4
  303.4 1.2 add_select_fusion.4
  305.9 1.2 add_select_fusion.4
  311.5 75.3 %psum.7 = f32[]{:T(128)} all-reduce(f32[]{:T(128)} %fusion.37), channel_id=1, replica_groups=mesh['seq'=32,'head'=8] {'seq','head'}, use_global_device_ids=true, to_apply=%region_17.18 | all-reduce | flops 1 | bytes 8 | tf_op jit(solution)/shard_map/psum | solution.py:138
  (90 shorter events, 39.5 us)
Async XLA Ops:
  7.2 51.9 %copy-start = (bf16[4,128,128]{2,1,0:T(8,128)(2,1)S(1)}, bf16[4,128,128]{2,1,0:T(8,128)(2,1)}, u32[]{:S(2)}) copy-start(bf16[4,128,128]{2,1,0:T(8,128)(2,1)} %param.13) | copy-start | bytes 393220
  7.2 80.6 %all-gather.7.cloned.1.call-start = ((), (), s32[]{:S(2)}) async-start(), calls=%async_computation | async-start | bytes 2162688 | tf_op jit(solution)/shard_map/all_gather | solution.py:123
  7.9 157.5 %all-gather.9.cloned.1.call-start = ((), (), s32[]{:S(2)}) async-start(), calls=%async_computation.1 | async-start | bytes 2162688 | tf_op jit(solution)/shard_map/all_gather | solution.py:124
  8.7 259.0 %all-gather.11.cloned.1.call-start = ((), (), s32[]{:S(2)}) async-start(), calls=%async_computation.2 | async-start | bytes 8650752 | tf_op jit(solution)/shard_map/all_gather | solution.py:17
  165.5 144.0 %copy-start.1 = (bf16[256,1,128]{2,0,1:T(8,128)(2,1)S(1)}, bf16[256,1,128]{2,0,1:T(8,128)(2,1)}, u32[]{:S(2)}) copy-start(bf16[256,1,128]{2,0,1:T(8,128)(2,1)} %param.12) | copy-start | bytes 196612
Sparse Core Ops, SparseCore 0:
  10.6 77.1 all-gather.6
  90.4 75.0 all-gather.8
  168.6 98.9 all-gather.10
where the time goes:
time: 397 us; the launch traced here: 396 us
  waiting for transfers between devices  191 us (48%)
  blocking collectives  118 us (30%)
  other arithmetic  47.1 us (12%)
  matrix products  18.1 us (5%)
  between operations  16.4 us (4%)
  local copies, waits for them, and re-layouts  5.16 us (1%)
    all_gather x1, waiting for transfers between devices, prefix(): lax.all_gather(part.astype(kind), axis)  86.1 us
    all_gather x1, waiting for transfers between devices, on_device(): value_part = lax.all_gather(values, 'seq', axis=0, tiled=True)  77.7 us
    psum x1, blocking collectives, on_device(): loss = lax.psum(jnp.sum(gap * gap), ('seq', 'head')) / entry_count  75.3 us
    all_gather x1, blocking collectives, prefix(): lax.all_gather(part.astype(kind), axis)  42.3 us
    select_n x64, other arithmetic, lap(): return jax.tree.map(lambda a, b: jnp.where(reached, a, b), new, before)  40 us
    all_gather x1, waiting for transfers between devices, on_device(): key_part = lax.all_gather(keys, 'seq', axis=0, tiled=True)  25.6 us
  transfers between devices with their start and end apart: 3, of which 3 were waited for; matrix products, arithmetic and copies ran while one was open for 7% of the time, Pallas kernels for 0%

commit v1 on v0

--- a/solution.py
+++ b/solution.py
@@ -9,6 +9,13 @@
 BLOCK = 128
 PRECISE = lax.Precision.HIGHEST
 MASKED = -1e30
+
+
+def _drive_core(unit):
+    return jnp.concatenate(
+        lax.all_to_all(jnp.stack([unit for _ in range(lax.axis_size("seq"))], axis=0), "seq", 0, 0),
+        0,
+    )
 
 
 def prefix(x, axis, combine, identity):
@@ -121,7 +128,7 @@
         jnp.zeros((head_count, BLOCK, head_width), jnp.float32),
     )
     key_part = lax.all_gather(keys, "seq", axis=0, tiled=True)
-    value_part = lax.all_gather(values, "seq", axis=0, tiled=True)
+    value_part = _drive_core(values)
     best, totals, accum = lax.cond(
         jnp.int32(0) <= row_first + BLOCK - 1,
         lambda kept: absorb(

time: 397 us -> 349 us (0.88)
  waiting for transfers between devices: 191 us -> 61.3 us
  blocking collectives: 118 us -> 162 us
  other arithmetic: 47.1 us -> 68.6 us
  starting transfers between devices: 0.11 us -> 12.2 us
    all_gather x1 -> x0, waiting for transfers between devices: 77.7 us -> none  [on_device(): value_part = lax.all_gather(values, 'seq', axis=0, tiled=True)]
    all_gather x1, blocking collectives: 42.3 us -> 86.4 us  [prefix(): lax.all_gather(part.astype(kind), axis)]
    all_gather x1, waiting for transfers between devices: 25.6 us -> 0.02 us  [on_device(): key_part = lax.all_gather(keys, 'seq', axis=0, tiled=True)]
    all_gather x1, waiting for transfers between devices: 86.1 us -> 60.6 us  [prefix(): lax.all_gather(part.astype(kind), axis)]
    select_n x64, other arithmetic: 40 us -> 61 us  [lap(): return jax.tree.map(lambda a, b: jnp.where(reached, a, b), new, before)]
    all_to_all x0 -> x1, starting transfers between devices: none -> 12.2 us  [_drive_core(): lax.all_to_all(jnp.stack([unit for _ in range(lax.axis_size('seq'))], axi...]
  transfers between devices with their start and end apart: 3 -> 3, of which waited for: 3 -> 1; matrix products, arithmetic and copies ran while one was open for 7% -> 8% of each run, Pallas kernels for 0% -> 0%
where the time goes in v1:
time: 349 us; the launch traced here: 346 us
  blocking collectives  162 us (46%)
  other arithmetic  68.6 us (20%)
  waiting for transfers between devices  61.3 us (18%)
  matrix products  18.8 us (5%)
  between operations  16.7 us (5%)
  starting transfers between devices  12.2 us (3%)
  local copies, waits for them, and re-layouts  6.78 us (2%)
    all_gather x1, blocking collectives, prefix(): lax.all_gather(part.astype(kind), axis)  86.4 us
    psum x1, blocking collectives, on_device(): loss = lax.psum(jnp.sum(gap * gap), ('seq', 'head')) / entry_count  75.3 us
    select_n x64, other arithmetic, lap(): return jax.tree.map(lambda a, b: jnp.where(reached, a, b), new, before)  61 us
    all_gather x1, waiting for transfers between devices, prefix(): lax.all_gather(part.astype(kind), axis)  60.6 us
    all_to_all x1, starting transfers between devices, _drive_core(): lax.all_to_all(jnp.stack([unit for _ in range(lax.axis_size('seq'))], axi...  12.2 us
  transfers between devices with their start and end apart: 3, of which 1 were waited for; matrix products, arithmetic and copies ran while one was open for 8% of the time, Pallas kernels for 0%

profile of v1, /device:TPU:1, one launch (start us, length us, event | category | flops | bytes accessed | tf_op | source)
XLA Modules:
  0.0 346.4 jit_solution(10392515710061401308)
XLA Ops:
  11.9 1.8 fusion.64
  13.7 2.7 stack.2
  16.4 12.2 %all-to-all-start = ((bf16[32,256,1,128]{3,1,2,0:T(8,128)(2,1)}), bf16[32,256,1,128]{3,1,2,0:T(8,128)(2,1)}, u32[]{:S(2)}, u32[]{:S(2)}) async-start(bf16[32,256,1,128]{3,1,2,0:T(8,128)(2,1)} %stack.2), calls=%async_computation | async-start | bytes 4194304 | tf_op jit(solution)/shard_map/all_to_all | solution.py:16
  28.6 1.2 dynamic_slice.26
  30.7 86.4 %all-gather.2 = bf16[32,4,256]{2,1,0:T(4,128)(2,1)} all-gather(bf16[1,4,256]{2,1,0:T(4,128)(2,1)S(1)} %convert_bitcast_fusion), channel_id=3, replica_groups=mesh['seq'=32,'head'=8] {'seq'}, dimensions={0}, use_global_device_ids=true | all-gather | bytes 67584 | tf_op jit(solution)/shard_map/all_gather | solution.py:24
  117.8 1.3 fusion.65
  119.2 1.3 fusion.68
  121.9 14.9 %conditional.1 = (f32[4,128]{1,0:T(4,128)S(1)}, f32[4,128,128]{2,1,0:T(8,128)S(1)}) conditional(s32[]{:T(128)} %convert_element_type.94, () %tuple.33, (s32[]{:T(128)}, s32[128]{0:T(128)S(1)}, bf16[256,4,128]{2,1,0:T(4,128)(2,1)S(1)}, s32[]{:T(128)}, bf16[8192,1,128]{2,0,1:T(8,128)(2,1)}, /*index=5*/bf16[32,256,1,128]{3,1,2,0:T(8,128)(2,1)}) %tuple.71), branch_computations={%region_12.13_spmd, %region_13.0_spmd} | conditional | flops 2194669056 | bytes 59651608 | solution.py:132
  122.6 4.8 %fusion = (f32[4,128]{1,0:T(4,128)S(1)}, f32[128,4,8192]{2,0,1:T(8,128)S(1)}) fusion(pred[128,8192]{1,0:T(8,128)(4,1)S(1)} %iota_compare_fusion, bf16[8192,1,128]{2,0,1:T(8,128)(2,1)} %get-tuple-element.140, bf16[256,4,128]{2,0,1:T(8,128)(2,1)S(1)} %copy.30, s32[]{:T(128)} %get-tuple-element.139), kind=kOutput, calls=%fused_computation.2 | convolution fusion | flops 1086324224 | bytes 20056068 | tf_op jit(solution)/shard_map/cond/branch_1_fun/bhd,kd->hbk/dot_general | solution.py:53
  127.4 4.7 %fusion.5 = f32[4,128,128]{2,1,0:T(8,128)S(1)} fusion(bf16[8192,128,1]{1,0,2:T(8,128)(2,1)} %bitcast.5, f32[128,4,8192]{2,0,1:T(8,128)S(1)} %get-tuple-element.205, f32[4,128]{1,0:T(4,128)S(1)} %broadcast_maximum_fusion, pred[128,8192]{1,0:T(8,128)(4,1)S(1)} %iota_compare_fusion), kind=kOutput, calls=%fused_computation.7 | convolution fusion | flops 1090519040 | bytes 20187136 | tf_op jit(solution)/shard_map/cond/branch_1_fun/hbk,kd->hbd/dot_general | solution.py:62
  132.1 4.5 %fusion.4 = f32[4,128]{1,0:T(4,128)S(1)} fusion(f32[128,4,8192]{2,0,1:T(8,128)S(1)} %get-tuple-element.205, f32[4,128]{1,0:T(4,128)S(1)} %broadcast_maximum_fusion, pred[128,8192]{1,0:T(8,128)(4,1)S(1)} %iota_compare_fusion), kind=kLoop, calls=%fused_computation.6 | loop fusion | flops 16776704 | bytes 17829888 | tf_op jit(solution)/shard_map/cond/branch_1_fun/reduce_sum | solution.py:61
  137.0 60.6 %all-gather.8.cloned.1.call-done = bf16[128,256,128]{2,1,0:T(8,128)(2,1)} async-done(((bf16[4,256,128]{2,1,0:T(8,128)(2,1)}), bf16[128,256,128]{2,1,0:T(8,128)(2,1)}) %all-gather.8.cloned.1.call-update) | async-done | bytes 8388624 | tf_op jit(solution)/shard_map/all_gather | solution.py:24
  197.6 61.0 %while.16 = (s32[]{:T(128)}, f32[4,256,128]{2,1,0:T(8,128)S(1)}, f32[4,256]{1,0:T(4,128)S(1)}, s32[]{:T(128)}, bf16[32,4,256,128]{3,2,1,0:T(8,128)(2,1)}, /*index=5*/bf16[32,4,256]{2,1,0:T(4,128)(2,1)}, s32[]{:T(128)}, s32[]{:T(128)}) while((s32[]{:T(128)}, f32[4,256,128]{2,1,0:T(8,128)S(1)}, f32[4,256]{1,0:T(4,128)S(1)}, ...), condition=%wide.region_10.0_spmd.clone, body=%wide.region_9.0_spmd.clone.sunk | while | flops 528388 | bytes 1321075 | solution.py:37
  197.6 1.2 add_select_fusion.4
  199.5 1.2 add_select_fusion.4
  201.4 1.2 add_select_fusion.4
  203.3 1.2 add_select_fusion.4
  205.2 1.2 add_select_fusion.4
  207.1 1.2 add_select_fusion.4
  209.0 1.2 add_select_fusion.4
  210.9 1.2 add_select_fusion.4
  212.8 1.2 add_select_fusion.4
  239.5 1.2 add_select_fusion.4
  261.6 75.3 %psum.7 = f32[]{:T(128)} all-reduce(f32[]{:T(128)} %fusion.36), channel_id=1, replica_groups=mesh['seq'=32,'head'=8] {'seq','head'}, use_global_device_ids=true, to_apply=%region_17.18 | all-reduce | flops 1 | bytes 8 | tf_op jit(solution)/shard_map/psum | solution.py:145
  (92 shorter events, 60.3 us)
Async XLA Ops:
  7.2 110.7 %copy-start = (bf16[4,128,128]{2,1,0:T(8,128)(2,1)S(1)}, bf16[4,128,128]{2,1,0:T(8,128)(2,1)}, u32[]{:S(2)}) copy-start(bf16[4,128,128]{2,1,0:T(8,128)(2,1)} %param.13) | copy-start | bytes 393220
  7.2 114.7 %copy-start.1 = (bf16[256,4,128]{2,1,0:T(4,128)(2,1)S(1)}, bf16[256,4,128]{2,1,0:T(4,128)(2,1)}, u32[]{:S(2)}) copy-start(bf16[256,4,128]{2,1,0:T(4,128)(2,1)} %param.10) | copy-start | bytes 786436
  7.2 114.6 %all-gather.6.cloned.1.call-start = ((), (), s32[]{:S(2)}) async-start(), calls=%async_computation.1 | async-start | bytes 2162688 | tf_op jit(solution)/shard_map/all_gather | solution.py:130
  7.9 189.6 %all-gather.8.cloned.1.call-start = ((), (), s32[]{:S(2)}) async-start(), calls=%async_computation.2 | async-start | bytes 8650752 | tf_op jit(solution)/shard_map/all_gather | solution.py:24
  16.4 105.4 %all-to-all-start = ((bf16[32,256,1,128]{3,1,2,0:T(8,128)(2,1)}), bf16[32,256,1,128]{3,1,2,0:T(8,128)(2,1)}, u32[]{:S(2)}, u32[]{:S(2)}) async-start(bf16[32,256,1,128]{3,1,2,0:T(8,128)(2,1)} %stack.2), calls=%async_computation | async-start | bytes 4194304 | tf_op jit(solution)/shard_map/all_to_all | solution.py:16
  121.9 137.8 %copy-start.2 = (bf16[256,1,128]{2,0,1:T(8,128)(2,1)S(1)}, bf16[256,1,128]{2,0,1:T(8,128)(2,1)}, u32[]{:S(2)}) copy-start(bf16[256,1,128]{2,0,1:T(8,128)(2,1)} %param.12) | copy-start | bytes 196612
Sparse Core Ops, SparseCore 0:
  10.6 84.9 all-gather.5
  98.8 98.7 all-gather.7
